TPU v7x, 32 devices: a whole 2x2x4 slice. The times are simulated.
32 devices in a mesh: groups: 2 (over y), tensor: 4 (over z), dp: 4 (over x, core).
Axes of the slice: x: 2, y: 2, z: 4, core: 2. Of those that a mesh axis runs over, the one named last changes fastest.
Arguments:
- root_features: bfloat16 [32, 16384], P('groups', 'dp'), parts along dimension 0, may hold values from -6 to 6
- branch_embeds: bfloat16 [32, 4, 8, 16384], P('groups', None, None, 'dp'), parts along dimension 0, may hold values from -6 to 6
- parents: int32 [32, 3, 8], P('groups'), parts along dimension 0, may hold values from 0 to 7
- cache_lengths: int32 [32], P(('groups', 'dp')), parts along dimension 0, may hold values from 128 to 512, as said below
- cache_kv: bfloat16 [32, 2, 512, 512], P(('groups', 'dp'), None, None, 'tensor'), parts along dimension 0, may hold values from -6 to 6, as said below
- norm_gain: bfloat16 [16384], P('dp'), may hold values from 0.099609375 to 1.8984375
- w_query: bfloat16 [16384, 2048], P('dp', 'tensor'), may hold values from -1 to 1
- w_keyval: bfloat16 [16384, 2, 512], P('dp', None, 'tensor'), may hold values from -1 to 1, as said below
- w_out: bfloat16 [2048, 16384], P('tensor', 'dp'), may hold values from -0.125 to 0.125
Outputs:
- tree_features: bfloat16 [32, 4, 8, 16384], P('groups', None, None, ('dp', 'tensor')), parts along dimension 0
There are 2 independent parts, one for each index of `groups`. A program takes and returns all parts, laid end to end along the dimension named above; an argument that names none is the same for every part. Nothing has to cross between parts.
Inputs may be any that keep to these rules, and one draw needn't show every extreme that they name: `cache_lengths`: some request has exactly 512 valid cache positions and some other exactly 128. `cache_kv`: for each request, keys and values, the 4 blocks of 128 columns k * 4 .. (k + 1) * 4 - 1 are equal; they hold key-value head k. `w_keyval`: for keys and values, the 4 blocks of 128 columns k * 4 .. (k + 1) * 4 - 1 are equal; they hold key-value head k.
All inputs are finite; a program needn't handle non-finite values.
Results may differ from a plain program's by a relative error of at most 0.017.
Values may be sent and summed in bfloat16 or wider, within the bound.
A program may use at most 128 MiB of HBM per device.

v0:
```python
import functools

import jax
import jax.numpy as jnp
from jax import lax
from jax.experimental import pallas as pl
from jax.experimental.pallas import tpu as pltpu
from jax.sharding import PartitionSpec as P

D = 16384
HD = 128
BRANCH = 8
DEPTHS = 4
CACHE = 512
BATCHES = 2
SUBS = 2


epsilon = 1e-05
masked_score = -1e30


def ancestor_path(parent_table, tree_level):
    current = jnp.broadcast_to(
        jnp.arange(BRANCH, dtype=jnp.int32)[None, :], (parent_table.shape[0], BRANCH)
    )
    path_nodes = [current]
    for upper in range(tree_level, 0, -1):
        current = jnp.take_along_axis(parent_table[:, upper - 1], current, axis=1)
        path_nodes.append(current)
    return path_nodes[::-1]


def tree_mask_of(parent_table, tree_level):
    path_nodes = ancestor_path(parent_table, tree_level)
    columns = jnp.arange(BRANCH, dtype=jnp.int32)
    blocks = []
    for other_level in range(DEPTHS):
        if other_level <= tree_level:
            blocks.append(columns[None, None, :] == path_nodes[other_level][:, :, None])
        else:
            blocks.append(jnp.zeros((parent_table.shape[0], BRANCH, BRANCH), dtype=bool))
    return jnp.concatenate(blocks, axis=2)


def shards(
    root_features,
    branch_embeds,
    parents,
    cache_lengths,
    cache_kv,
    norm_gain,
    w_query,
    w_keyval,
    w_out,
):
    request_count, feat_cols = root_features.shape
    local_requests = cache_lengths.shape[0]
    head_cols = w_query.shape[1]
    kv_cols = w_keyval.shape[2]
    kv_local = kv_cols // HD
    all_rows = request_count * BRANCH
    own_rows = local_requests * BRANCH
    share_cols = feat_cols // lax.axis_size("tensor")
    dp_index = lax.axis_index("dp")
    tensor_index = lax.axis_index("tensor")
    weights = jnp.concatenate([w_query, w_keyval.reshape(feat_cols, 2 * kv_cols)], axis=1)
    gain = norm_gain.astype(jnp.float32)
    own_parents = lax.dynamic_slice_in_dim(parents, dp_index * local_requests, local_requests, 0)
    cache_keys = cache_kv[:, 0].reshape(local_requests, CACHE, kv_local, HD)
    cache_values = cache_kv[:, 1].reshape(local_requests, CACHE, kv_local, HD)
    positions = jnp.arange(CACHE, dtype=jnp.int32)
    cache_valid = positions[None, :] < cache_lengths[:, None]
    tree_keys = jnp.zeros((local_requests, DEPTHS * BRANCH, kv_local, HD), jnp.bfloat16)
    tree_values = jnp.zeros((local_requests, DEPTHS * BRANCH, kv_local, HD), jnp.bfloat16)
    results = []
    previous = None
    for tree_level in range(DEPTHS):
        if tree_level == 0:
            parent = jnp.broadcast_to(root_features[:, None, :], (request_count, BRANCH, feat_cols))
        else:
            parent = jnp.take_along_axis(previous, parents[:, tree_level - 1][:, :, None], axis=1)
        node_state = parent.astype(jnp.float32) + branch_embeds[:, tree_level].astype(jnp.float32)
        flat_state = node_state.reshape(all_rows, feat_cols)
        square_sums = jnp.sum(flat_state * flat_state, axis=1)
        scaled = (flat_state * gain).astype(jnp.bfloat16)
        total_sums = lax.psum(square_sums, "dp")
        own_sums = lax.dynamic_slice_in_dim(total_sums, dp_index * own_rows, own_rows, 0)
        proj_terms = lax.psum_scatter(
            jnp.dot(scaled, weights, preferred_element_type=jnp.float32).astype(jnp.bfloat16),
            "dp",
            scatter_dimension=0,
            tiled=True,
        ).astype(jnp.float32)
        inv_rms = lax.rsqrt(own_sums / D + epsilon)[:, None]
        projected = (proj_terms * inv_rms).astype(jnp.bfloat16)
        queries = projected[:, :head_cols].reshape(local_requests, BRANCH, kv_local, -1, HD)
        new_keys = projected[:, head_cols : head_cols + kv_cols].reshape(
            local_requests, BRANCH, kv_local, HD
        )
        new_values = projected[:, head_cols + kv_cols :].reshape(
            local_requests, BRANCH, kv_local, HD
        )
        tree_keys = tree_keys.at[:, tree_level * BRANCH : (tree_level + 1) * BRANCH].set(new_keys)
        tree_values = tree_values.at[:, tree_level * BRANCH : (tree_level + 1) * BRANCH].set(
            new_values
        )
        tree_mask = tree_mask_of(own_parents, tree_level)
        cache_scores = jnp.einsum(
            "rbkgd,rckd->rkgbc", queries, cache_keys, preferred_element_type=jnp.float32
        ) * HD ** (-0.5)
        tree_scores = jnp.einsum(
            "rbkgd,rtkd->rkgbt", queries, tree_keys, preferred_element_type=jnp.float32
        ) * HD ** (-0.5)
        cache_scores = jnp.where(cache_valid[:, None, None, None, :], cache_scores, masked_score)
        tree_scores = jnp.where(tree_mask[:, None, None, :, :], tree_scores, masked_score)
        row_max = jnp.maximum(jnp.max(cache_scores, axis=4), jnp.max(tree_scores, axis=4))[
            ..., None
        ]
        cache_exp = jnp.exp(cache_scores - row_max)
        tree_exp = jnp.exp(tree_scores - row_max)
        denominator = jnp.sum(cache_exp, axis=4, keepdims=True) + jnp.sum(
            tree_exp, axis=4, keepdims=True
        )
        cache_weights = (cache_exp / denominator).astype(jnp.bfloat16)
        tree_weights = (tree_exp / denominator).astype(jnp.bfloat16)
        mixed = jnp.einsum(
            "rkgbc,rckd->rbkgd", cache_weights, cache_values, preferred_element_type=jnp.float32
        )
        mixed = mixed + jnp.einsum(
            "rkgbt,rtkd->rbkgd", tree_weights, tree_values, preferred_element_type=jnp.float32
        )
        attended = mixed.reshape(own_rows, head_cols).astype(jnp.bfloat16)
        partial_out = jnp.dot(
            lax.all_gather(attended, "dp", axis=0, tiled=True),
            w_out,
            preferred_element_type=jnp.float32,
        )
        share_sums = lax.psum_scatter(
            partial_out.astype(jnp.bfloat16), "tensor", scatter_dimension=1, tiled=True
        ).astype(jnp.float32)
        residual = lax.dynamic_slice_in_dim(flat_state, tensor_index * share_cols, share_cols, 1)
        fresh_share = (residual + share_sums).astype(jnp.bfloat16)
        if tree_level + 1 < DEPTHS:
            gathered = lax.all_gather(fresh_share, "tensor", axis=1, tiled=True)
            previous = gathered.reshape(request_count, BRANCH, feat_cols)
        results.append(fresh_share.reshape(request_count, BRANCH, share_cols))
    return jnp.stack(results, axis=1)


MESH = pl.DeviceIdType.MESH


def dot32(a, b):
    return jnp.dot(a, b, preferred_element_type=jnp.float32)


def dot32_t(a, b):
    return lax.dot_general(a, b, (((1,), (1,)), ((), ())), preferred_element_type=jnp.float32)


def tree_kernel(
    n,
    m,
    root_ref,
    emb_hbm,
    hot_ref,
    len_ref,
    cache_hbm,
    gain_ref,
    wq_hbm,
    wkv_hbm,
    wo_hbm,
    out_ref,
    emb0,
    emb_share,
    cache,
    wq,
    wkv,
    wo,
    scaled,
    share_sums,
    state,
    proj,
    proj_send,
    proj_recv,
    sums_send,
    sums_recv,
    tree_keys,
    tree_values,
    tree_mask,
    att,
    part,
    rs_send,
    rs_recv,
    total,
    load_sem,
    ag_ssem,
    ag_rsem,
    tsum_ssem,
    tsum_rsem,
    proj_ssem,
    proj_rsem,
    dsum_ssem,
    dsum_rsem,
    att_ssem,
    att_rsem,
    rs_ssem,
    rs_rsem,
):
    t = lax.axis_index("tensor")
    d = lax.axis_index("dp")
    requests, feat = root_ref.shape
    own_requests = requests // m
    part_requests = own_requests // BATCHES
    own = part_requests * BRANCH
    rows = own * m
    lanes = sums_send.shape[2]
    share = feat // n
    head_cols = wq.shape[1]
    heads = head_cols // HD
    steps = BATCHES * DEPTHS

    sub = share // SUBS

    def sub_of(s, u):
        return pl.ds(pl.multiple_of(s * share + u * sub, sub), sub)

    def cols_of(s):
        return pl.ds(pl.multiple_of(s * share, share), share)

    def batch_rows(b):
        return [pl.ds(k * own_requests + b * part_requests, part_requests) for k in range(m)]

    def joined(blocks, columns):
        return jnp.concatenate(blocks, axis=0).astype(jnp.float32).reshape(rows, columns)

    loads = [
        pltpu.make_async_copy(emb_hbm.at[:, 0], emb0, load_sem.at[0]),
        pltpu.make_async_copy(wq_hbm, wq, load_sem.at[1]),
        pltpu.make_async_copy(wkv_hbm, wkv, load_sem.at[2]),
        pltpu.make_async_copy(cache_hbm, cache, load_sem.at[3]),
        pltpu.make_async_copy(wo_hbm, wo, load_sem.at[4]),
    ]
    for e in range(1, DEPTHS):
        loads.append(
            pltpu.make_async_copy(
                emb_hbm.at[:, e, :, cols_of(t)], emb_share.at[e - 1], load_sem.at[4 + e]
            )
        )
    for load in loads:
        load.start()

    dp_to = [lax.rem(d + k, m) for k in range(1, m)]
    t_to = [lax.rem(t + k, n) for k in range(1, n)]

    barrier = pltpu.get_barrier_semaphore()
    for peer in dp_to:
        pl.semaphore_signal(barrier, inc=1, device_id={"dp": peer}, device_id_type=MESH)
    for peer in t_to:
        pl.semaphore_signal(barrier, inc=1, device_id={"tensor": peer}, device_id_type=MESH)
    pl.semaphore_wait(barrier, m + n - 2)

    def ag_copy(e, s, u, to, send_slot):
        return pltpu.make_async_remote_copy(
            src_ref=scaled.at[e, s, u],
            dst_ref=scaled.at[e, s, u],
            send_sem=ag_ssem.at[e, send_slot, u],
            recv_sem=ag_rsem.at[e, s, u],
            device_id={"tensor": to},
            device_id_type=MESH,
        )

    def tsum_copy(e, k):
        return pltpu.make_async_remote_copy(
            src_ref=share_sums.at[e, n - 1],
            dst_ref=share_sums.at[e, k],
            send_sem=tsum_ssem.at[e, k],
            recv_sem=tsum_rsem.at[e, k],
            device_id={"tensor": t_to[k]},
            device_id_type=MESH,
        )

    def proj_copy(e, k):
        return pltpu.make_async_remote_copy(
            src_ref=proj_send.at[e, dp_to[k]],
            dst_ref=proj_recv.at[e, k],
            send_sem=proj_ssem.at[e, k],
            recv_sem=proj_rsem.at[e, k],
            device_id={"dp": dp_to[k]},
            device_id_type=MESH,
        )

    def dsum_copy(e, k):
        return pltpu.make_async_remote_copy(
            src_ref=sums_send.at[e],
            dst_ref=sums_recv.at[e, k],
            send_sem=dsum_ssem.at[e, k],
            recv_sem=dsum_rsem.at[e, k],
            device_id={"dp": dp_to[k]},
            device_id_type=MESH,
        )

    def att_copy(e, k):
        return pltpu.make_async_remote_copy(
            src_ref=att.at[e, d],
            dst_ref=att.at[e, d],
            send_sem=att_ssem.at[e, k],
            recv_sem=att_rsem.at[e, k],
            device_id={"dp": dp_to[k]},
            device_id_type=MESH,
        )

    def rs_copy(e, s, u, to, slot):
        return pltpu.make_async_remote_copy(
            src_ref=rs_send.at[e, s, u],
            dst_ref=rs_recv.at[e, slot, u],
            send_sem=rs_ssem.at[e, s, u],
            recv_sem=rs_rsem.at[e, slot, u],
            device_id={"tensor": to},
            device_id_type=MESH,
        )

    def rs_right(e, s, u):
        return rs_copy(e, s, u, t + 1, s)

    def rs_left(e, s, u):
        return rs_copy(e, s, u, t - 1, jnp.where(t - 1 == s, n, s))

    def rs_wait(e, slot, u):
        rs_copy(e, 0, u, lax.rem(t + 1, n), slot).wait_recv()

    eye = lax.broadcasted_iota(jnp.int32, (rows, lanes), 0) == lax.broadcasted_iota(
        jnp.int32, (rows, lanes), 1
    )

    def to_lanes(column):
        spread = jnp.where(eye, jnp.broadcast_to(column, (rows, lanes)), 0.0)
        return jnp.broadcast_to(jnp.sum(spread, axis=0, keepdims=True), (8, lanes))

    def product(i, s, first=False):
        for u in range(SUBS):
            block = scaled[i, s, u]
            cols = sub_of(s, u)
            if first and u == 0:
                proj[:, :head_cols] = dot32(block, wq[cols])
                proj[:, head_cols:] = dot32(block, wkv[cols])
            else:
                proj[:, :head_cols] += dot32(block, wq[cols])
                proj[:, head_cols:] += dot32(block, wkv[cols])

    def gather_wave(i, k):
        before = t - k
        after = t + k

        for u in range(SUBS):

            @pl.when(before >= 0)
            def _():
                ag_copy(i, before, u, lax.rem(t + 1, n), before).wait_recv()

                @pl.when(t < n - 1)
                def _():
                    ag_copy(i, before, u, t + 1, before).start()

            @pl.when(after < n)
            def _():
                ag_copy(i, after, u, lax.rem(t + 1, n), after).wait_recv()

                @pl.when(t > 0)
                def _():
                    ag_copy(i, after, u, t - 1, after).start()

        @pl.when(before >= 0)
        def _():
            product(i, before)

        @pl.when(after < n)
        def _():
            product(i, after)

    def add_arrived(i, s, u):
        rs_wait(i, s, u)
        rs_send[i, s, u] = (part[s, u] + rs_recv[i, s, u].astype(jnp.float32)).astype(
            jnp.bfloat16
        )

    def sum_wave(i, w, u):
        right = n - 1 + t - w
        left = w - (n - 1 - t)

        @pl.when((t > 0) & (right <= n - 1) & (right > t))
        def _():
            add_arrived(i, right, u)
            rs_right(i, right, u).start()

        @pl.when((t < n - 1) & (left >= 0) & (left < t))
        def _():
            add_arrived(i, left, u)
            rs_left(i, left, u).start()

    def later_waves(i):
        for u in range(SUBS):
            for w in range(1 if u else 2, n - 1):
                sum_wave(i, w, u)

    def finish(i):
        b = lax.rem(i, BATCHES)
        e = i // BATCHES
        later = i + BATCHES
        more = e < DEPTHS - 1
        for u in range(SUBS):
            cols = slice(u * sub, (u + 1) * sub)
            total[u] = state[b, u] + part[t, u]

            @pl.when(t > 0)
            def _():
                rs_wait(i, t, u)
                total[u] += rs_recv[i, t, u].astype(jnp.float32)

            @pl.when(t < n - 1)
            def _():
                rs_wait(i, n, u)
                total[u] += rs_recv[i, n, u].astype(jnp.float32)

            @pl.when(more)
            def _():
                embeds = joined([emb_share[e, r, :, cols] for r in batch_rows(b)], sub)
                node = dot32(hot_ref[i], total[u].astype(jnp.bfloat16)) + embeds
                state[b, u] = node
                scaled[later, t, u] = (node * gain_ref[:, sub_of(t, u)].astype(jnp.float32)).astype(jnp.bfloat16)

                @pl.when(t < n - 1)
                def _():
                    ag_copy(later, t, u, t + 1, t).start()

                @pl.when(t > 0)
                def _():
                    ag_copy(later, t, u, t - 1, n).start()

        @pl.when(more)
        def _():
            squares = jnp.zeros((rows, 1), jnp.float32)
            for u in range(SUBS):
                node = state[b, u]
                squares = squares + jnp.sum(node * node, axis=1, keepdims=True)
            share_sums[later, n - 1] = to_lanes(squares)
            for k in range(n - 1):
                tsum_copy(later, k).start()

        for u in range(SUBS):
            for k, r in enumerate(batch_rows(b)):
                out_ref[r, pl.ds(e, 1), :, u * sub : (u + 1) * sub] = (
                    total[u, k * own : (k + 1) * own]
                    .reshape(part_requests, 1, BRANCH, sub)
                    .astype(jnp.bfloat16)
                )

    row_id = lax.broadcasted_iota(jnp.int32, (rows, requests), 0)
    request_id = lax.broadcasted_iota(jnp.int32, (rows, requests), 1)
    loads[0].wait()

    def first_states(b, carry):
        place = row_id // BRANCH
        request = (
            place // part_requests * own_requests + b * part_requests + place % part_requests
        )
        root_hot = (request == request_id).astype(jnp.bfloat16)
        squares = jnp.zeros((rows, 1), jnp.float32)
        for s in range(n):
            cols = slice(s * share, (s + 1) * share)
            embeds = joined([emb0[r, :, cols] for r in batch_rows(b)], share)
            node = dot32(root_hot, root_ref[:, cols]) + embeds
            squares = squares + jnp.sum(node * node, axis=1, keepdims=True)
            fed = (node * gain_ref[:, cols].astype(jnp.float32)).astype(jnp.bfloat16)
            for u in range(SUBS):
                scaled[b, s, u] = fed[:, u * sub : (u + 1) * sub]

            @pl.when(t == s)
            def _():
                for u in range(SUBS):
                    state[b, u] = node[:, u * sub : (u + 1) * sub]

        sums_send[b] = to_lanes(squares)
        return carry

    lax.fori_loop(0, BATCHES, first_states, 0)
    tree_keys[...] = jnp.zeros_like(tree_keys)
    tree_values[...] = jnp.zeros_like(tree_values)
    tree_mask[...] = jnp.zeros_like(tree_mask)
    loads[1].wait()
    loads[2].wait()

    def step(i, carry):
        b = lax.rem(i, BATCHES)
        e = i // BATCHES
        later = i + BATCHES - 1
        gathering = (i > 0) & (later < steps)

        @pl.when(e == 0)
        def _():
            product(i, 0, True)
            for s in range(1, n):
                product(i, s)

        @pl.when(e > 0)
        def _():
            gather_wave(i, n - 1)
            summed = share_sums[i, n - 1]
            for k in range(n - 1):
                tsum_copy(i, k).wait_recv()
                summed = summed + share_sums[i, k]
            sums_send[i] = summed

        for k in range(m):
            proj_send[i, k] = proj[k * own : (k + 1) * own].astype(jnp.bfloat16)
        for k in range(m - 1):
            proj_copy(i, k).start()
            dsum_copy(i, k).start()

        @pl.when(i > 0)
        def _():
            later_waves(i - 1)

        own_row = lax.broadcasted_iota(jnp.int32, (own, DEPTHS * own), 0)
        own_col = lax.broadcasted_iota(jnp.int32, (own, DEPTHS * own), 1)
        itself = (own_col == own_row + e * own).astype(jnp.float32)
        own_rows = pl.ds(pl.multiple_of(d * own, own), own)
        mask_now = itself + dot32(hot_ref[jnp.maximum(i - BATCHES, 0), own_rows], tree_mask[b])
        tree_mask[b, own_rows] = mask_now.astype(jnp.bfloat16)

        projected = proj[pl.ds(pl.multiple_of(d * own, own), own)]
        summed = sums_send[i]
        for k in range(m - 1):
            proj_copy(i, k).wait_recv()
            dsum_copy(i, k).wait_recv()
            projected = projected + proj_recv[i, k].astype(jnp.float32)
            summed = summed + sums_recv[i, k]
        pick = lax.broadcasted_iota(jnp.int32, (own, lanes), 1) == (
            lax.broadcasted_iota(jnp.int32, (own, lanes), 0) + d * own
        )
        own_sums = jnp.sum(
            jnp.where(pick, jnp.broadcast_to(summed[0:1], (own, lanes)), 0.0),
            axis=1,
            keepdims=True,
        )
        inv_rms = lax.rsqrt(own_sums / (feat * m) + epsilon)
        projected = projected * inv_rms
        queries = jnp.concatenate(
            [
                projected[:, h * HD : (h + 1) * HD].reshape(part_requests, 1, BRANCH, HD)
                for h in range(heads)
            ],
            axis=1,
        ).reshape(own * heads, HD).astype(jnp.bfloat16)
        now = pl.ds(pl.multiple_of(e * own, own), own)
        tree_keys[b, now] = projected[:, head_cols : head_cols + HD].astype(jnp.bfloat16)
        tree_values[b, now] = projected[:, head_cols + HD :].astype(jnp.bfloat16)

        @pl.when(i == 0)
        def _():
            loads[3].wait()

        per = heads * BRANCH
        tree_scores = dot32_t(queries, tree_keys[b]) * HD ** (-0.5)
        allowed = jnp.broadcast_to(
            mask_now.reshape(part_requests, 1, BRANCH, DEPTHS * own),
            (part_requests, heads, BRANCH, DEPTHS * own),
        ).reshape(own * heads, DEPTHS * own)
        tree_scores = jnp.where(allowed > 0.5, tree_scores, masked_score)
        cache_scores = []
        position = lax.broadcasted_iota(jnp.int32, (per, CACHE), 1)
        for r in range(part_requests):
            request = b * part_requests + r
            scores = dot32_t(queries[r * per : (r + 1) * per], cache[request, 0]) * HD ** (-0.5)
            cache_scores.append(jnp.where(position < len_ref[request], scores, masked_score))
        cache_scores = jnp.concatenate(cache_scores, axis=0)
        row_max = jnp.maximum(
            jnp.max(cache_scores, axis=1, keepdims=True),
            jnp.max(tree_scores, axis=1, keepdims=True),
        )
        cache_exp = jnp.exp(cache_scores - row_max)
        tree_exp = jnp.exp(tree_scores - row_max)
        denominator = jnp.sum(cache_exp, axis=1, keepdims=True) + jnp.sum(
            tree_exp, axis=1, keepdims=True
        )
        cache_weights = (cache_exp / denominator).astype(jnp.bfloat16)
        tree_weights = (tree_exp / denominator).astype(jnp.bfloat16)
        mixed = jnp.concatenate(
            [
                dot32(cache_weights[r * per : (r + 1) * per], cache[b * part_requests + r, 1])
                for r in range(part_requests)
            ],
            axis=0,
        ) + dot32(tree_weights, tree_values[b])
        mixed = mixed.reshape(part_requests, heads, BRANCH, HD)
        for h in range(heads):
            att[i, d, :, h * HD : (h + 1) * HD] = mixed[:, h].reshape(own, HD).astype(jnp.bfloat16)
        for k in range(m - 1):
            att_copy(i, k).start()

        @pl.when(i > 0)
        def _():
            finish(i - 1)

        @pl.when(gathering)
        def _():
            product(later, t, True)

        for k in range(m - 1):
            att_copy(i, k).wait_recv()

        @pl.when(i == 0)
        def _():
            for load in loads[4:]:
                load.wait()

        attended = att[i].reshape(rows, head_cols)
        for u in range(SUBS):
            done = set()
            for k in range(n):
                right, left = n - 1 - k, k
                for s in (right, left):
                    if s not in done:
                        low = s * share + u * sub
                        part[s, u] = dot32(attended, wo[:, low : low + sub])
                        done.add(s)
                if k < n - 1:

                    @pl.when(t == 0)
                    def _():
                        rs_send[i, right, u] = part[right, u].astype(jnp.bfloat16)
                        rs_right(i, right, u).start()

                    @pl.when(t == n - 1)
                    def _():
                        rs_send[i, left, u] = part[left, u].astype(jnp.bfloat16)
                        rs_left(i, left, u).start()

        if n > 2:

            @pl.when(gathering)
            def _():
                gather_wave(later, 1)

            sum_wave(i, 1, 0)

            @pl.when(gathering)
            def _():
                for k in range(2, n - 1):
                    gather_wave(later, k)

        return carry

    lax.fori_loop(0, steps, step, 0)
    later_waves(steps - 1)
    finish(steps - 1)

    def drain(i, carry):
        for k in range(m - 1):
            proj_copy(i, k).wait_send()
            dsum_copy(i, k).wait_send()
            att_copy(i, k).wait_send()
        for u in range(SUBS):
            for s in range(n):

                @pl.when(t < s)
                def _():
                    rs_right(i, s, u).wait_send()

                @pl.when(t > s)
                def _():
                    rs_left(i, s, u).wait_send()

        @pl.when(i >= BATCHES)
        def _():
            for k in range(n - 1):
                tsum_copy(i, k).wait_send()
            for u in range(SUBS):
                for s in range(n):

                    @pl.when((s <= t) & (t < n - 1))
                    def _():
                        ag_copy(i, s, u, t + 1, s).wait_send()

                    @pl.when((s > t) & (t > 0))
                    def _():
                        ag_copy(i, s, u, t - 1, s).wait_send()

                @pl.when(t > 0)
                def _():
                    ag_copy(i, t, u, t - 1, n).wait_send()

        return carry

    lax.fori_loop(0, steps, drain, 0)


def kernel_shards(
    root_features,
    branch_embeds,
    parents,
    cache_lengths,
    cache_kv,
    norm_gain,
    w_query,
    w_keyval,
    w_out,
):
    n = lax.axis_size("tensor")
    m = lax.axis_size("dp")
    requests, feat = root_features.shape
    own_requests = cache_lengths.shape[0]
    part_requests = own_requests // BATCHES
    own = part_requests * BRANCH
    rows = own * m
    lanes = -(-rows // 128) * 128
    steps = BATCHES * DEPTHS
    share = feat // n
    head_cols = w_query.shape[1]
    proj_cols = head_cols + 2 * HD

    def one_hots(table):
        count = rows
        split = table.reshape(m, BATCHES, part_requests, DEPTHS - 1, BRANCH)
        split = jnp.transpose(split, (3, 1, 0, 2, 4)).reshape((DEPTHS - 1) * BATCHES, count)
        lane = jnp.arange(count, dtype=jnp.int32)
        index = split + (lane // BRANCH * BRANCH)[None, :]
        return (index[:, :, None] == lane[None, None, :]).astype(jnp.bfloat16)

    hot = one_hots(parents)
    bf16, f32 = jnp.bfloat16, jnp.float32
    vmem = pl.BlockSpec(memory_space=pltpu.VMEM)
    smem = pl.BlockSpec(memory_space=pltpu.SMEM)
    hbm = pl.BlockSpec(memory_space=pl.ANY)
    dma = pltpu.SemaphoreType.DMA
    return pl.pallas_call(
        functools.partial(tree_kernel, n, m),
        out_shape=jax.ShapeDtypeStruct((requests, DEPTHS, BRANCH, share), bf16),
        in_specs=[vmem, hbm, vmem, smem, hbm, vmem, hbm, hbm, hbm],
        out_specs=vmem,
        scratch_shapes=[
            pltpu.VMEM((requests, BRANCH, feat), bf16),
            pltpu.VMEM((DEPTHS - 1, requests, BRANCH, share), bf16),
            pltpu.VMEM(cache_kv.shape, bf16),
            pltpu.VMEM((feat, head_cols), bf16),
            pltpu.VMEM((feat, 2 * HD), bf16),
            pltpu.VMEM((head_cols, feat), bf16),
            pltpu.VMEM((steps, n, SUBS, rows, share // SUBS), bf16),
            pltpu.VMEM((steps, n, 8, lanes), f32),
            pltpu.VMEM((BATCHES, SUBS, rows, share // SUBS), f32),
            pltpu.VMEM((rows, proj_cols), f32),
            pltpu.VMEM((steps, m, own, proj_cols), bf16),
            pltpu.VMEM((steps, m - 1, own, proj_cols), bf16),
            pltpu.VMEM((steps, 8, lanes), f32),
            pltpu.VMEM((steps, m - 1, 8, lanes), f32),
            pltpu.VMEM((BATCHES, DEPTHS * own, HD), bf16),
            pltpu.VMEM((BATCHES, DEPTHS * own, HD), bf16),
            pltpu.VMEM((BATCHES, rows, DEPTHS * own), bf16),
            pltpu.VMEM((steps, m, own, head_cols), bf16),
            pltpu.VMEM((n, SUBS, rows, share // SUBS), f32),
            pltpu.VMEM((steps, n, SUBS, rows, share // SUBS), bf16),
            pltpu.VMEM((steps, n + 1, SUBS, rows, share // SUBS), bf16),
            pltpu.VMEM((SUBS, rows, share // SUBS), f32),
            dma((4 + DEPTHS,)),
            dma((steps, n + 1, SUBS)),
            dma((steps, n, SUBS)),
            dma((steps, n - 1)),
            dma((steps, n - 1)),
            dma((steps, m - 1)),
            dma((steps, m - 1)),
            dma((steps, m - 1)),
            dma((steps, m - 1)),
            dma((steps, m - 1)),
            dma((steps, m - 1)),
            dma((steps, n, SUBS)),
            dma((steps, n + 1, SUBS)),
        ],
        compiler_params=pltpu.CompilerParams(
            collective_id=0, has_side_effects=True, vmem_limit_bytes=60 * 1024 * 1024
        ),
    )(
        root_features,
        branch_embeds,
        hot,
        cache_lengths,
        cache_kv,
        norm_gain[None, :],
        w_query,
        w_keyval.reshape(feat, 2 * HD),
        w_out,
    )


def solution(mesh):
    in_line = 1 < mesh.shape["tensor"] <= 8 and mesh.shape["dp"] > 1
    return jax.shard_map(
        kernel_shards if in_line else shards,
        mesh=mesh,
        in_specs=(
            P("groups", "dp"),
            P("groups", None, None, "dp"),
            P("groups", None, None),
            P(("groups", "dp")),
            P(("groups", "dp"), None, None, "tensor"),
            P("dp"),
            P("dp", "tensor"),
            P("dp", None, "tensor"),
            P("tensor", "dp"),
        ),
        out_specs=P("groups", None, None, ("dp", "tensor")),
        check_vma=False,
    )
```

profile of v0, /device:TPU:0, one launch (start us, length us, event | category | flops | bytes accessed | tf_op | source)
XLA Modules:
  0.0 163.1 jit_solution(16117799610304709596)
XLA Ops:
  0.0 1.3 broadcast_in_dim.2.gain_ref
  1.3 0.8 copy.12
  2.1 0.1 reshape.41
  2.2 0.8 fusion.hot_ref
  3.0 3.2 %copy.16 = bf16[512,8,2,128]{3,1,2,0:T(8,128)(2,1)} copy(bf16[512,8,2,128]{3,2,1,0:T(2,128)(2,1)} %bitcast.8) | data formatting | bytes 4194304
  6.2 154.6 %shard_map.91 = bf16[16,4,8,1024]{3,2,1,0:T(8,128)(2,1)} custom-call(bf16[16,4096]{1,0:T(8,128)(2,1)} %root_ref.1, bf16[16,4,8,4096]{3,2,1,0:T(8,128)(2,1)} %emb_hbm.1, bf16[6,64,64]{2,1,0:T(8,128)(2,1)} %fusion.hot_ref, s32[4]{0:T(128)} %len_ref.1, bf16[4,2,512,128]{3,2,1,0:T(8,128)(2,1)} %cache_hbm.1, bf16[1,4096]{1,0:T(2,128)(2,1)} %broadcast_in_dim.2.gain_ref, ...), custom_call_target="tpu_custom_call" | custom-call | tf_op jit(solution)/shard_map/pallas_call | solution.py:737
  160.8 2.3 %copy.18 = bf16[16,4,8,1024]{3,2,1,0:T(8,128)(2,1)} copy(bf16[16,4,8,1024]{3,2,1,0:T(8,128)(2,1)} %shard_map.91) | data formatting | bytes 2097152
  (3 shorter events, 0.0 us)
where the time goes:
time: 163 us
  Pallas kernels  155 us (95%)
  local copies, waits for them, and re-layouts  7.69 us (5%)
    pallas_call x1, Pallas kernels, kernel_shards(): pl.pallas_call(functools.partial(tree_kernel, n, m), out_shape=jax.ShapeD...  155 us
    unnamed x3, local copies, waits for them, and re-layouts  6.28 us

commit v1 on v0

v1 whole, which is shorter than its diff:
```python
import functools

import jax
import jax.numpy as jnp
from jax import lax
from jax.experimental import pallas as pl
from jax.experimental.pallas import tpu as pltpu
from jax.sharding import PartitionSpec as P

D = 16384
HD = 128
BRANCH = 8
DEPTHS = 4
CACHE = 512
BATCHES = 2
PER = 4
HOP = 2.8
PACE = 0.65
PERIOD = 12.5
TURN = 7.2
PROJ_TRIP = 2.9
SLACK = 0.5


epsilon = 1e-05
masked_score = -1e30


def ancestor_path(parent_table, tree_level):
    current = jnp.broadcast_to(
        jnp.arange(BRANCH, dtype=jnp.int32)[None, :], (parent_table.shape[0], BRANCH)
    )
    path_nodes = [current]
    for upper in range(tree_level, 0, -1):
        current = jnp.take_along_axis(parent_table[:, upper - 1], current, axis=1)
        path_nodes.append(current)
    return path_nodes[::-1]


def tree_mask_of(parent_table, tree_level):
    path_nodes = ancestor_path(parent_table, tree_level)
    columns = jnp.arange(BRANCH, dtype=jnp.int32)
    blocks = []
    for other_level in range(DEPTHS):
        if other_level <= tree_level:
            blocks.append(columns[None, None, :] == path_nodes[other_level][:, :, None])
        else:
            blocks.append(jnp.zeros((parent_table.shape[0], BRANCH, BRANCH), dtype=bool))
    return jnp.concatenate(blocks, axis=2)


def shards(
    root_features,
    branch_embeds,
    parents,
    cache_lengths,
    cache_kv,
    norm_gain,
    w_query,
    w_keyval,
    w_out,
):
    request_count, feat_cols = root_features.shape
    local_requests = cache_lengths.shape[0]
    head_cols = w_query.shape[1]
    kv_cols = w_keyval.shape[2]
    kv_local = kv_cols // HD
    all_rows = request_count * BRANCH
    own_rows = local_requests * BRANCH
    share_cols = feat_cols // lax.axis_size("tensor")
    dp_index = lax.axis_index("dp")
    tensor_index = lax.axis_index("tensor")
    weights = jnp.concatenate([w_query, w_keyval.reshape(feat_cols, 2 * kv_cols)], axis=1)
    gain = norm_gain.astype(jnp.float32)
    own_parents = lax.dynamic_slice_in_dim(parents, dp_index * local_requests, local_requests, 0)
    cache_keys = cache_kv[:, 0].reshape(local_requests, CACHE, kv_local, HD)
    cache_values = cache_kv[:, 1].reshape(local_requests, CACHE, kv_local, HD)
    positions = jnp.arange(CACHE, dtype=jnp.int32)
    cache_valid = positions[None, :] < cache_lengths[:, None]
    tree_keys = jnp.zeros((local_requests, DEPTHS * BRANCH, kv_local, HD), jnp.bfloat16)
    tree_values = jnp.zeros((local_requests, DEPTHS * BRANCH, kv_local, HD), jnp.bfloat16)
    results = []
    previous = None
    for tree_level in range(DEPTHS):
        if tree_level == 0:
            parent = jnp.broadcast_to(root_features[:, None, :], (request_count, BRANCH, feat_cols))
        else:
            parent = jnp.take_along_axis(previous, parents[:, tree_level - 1][:, :, None], axis=1)
        node_state = parent.astype(jnp.float32) + branch_embeds[:, tree_level].astype(jnp.float32)
        flat_state = node_state.reshape(all_rows, feat_cols)
        square_sums = jnp.sum(flat_state * flat_state, axis=1)
        scaled = (flat_state * gain).astype(jnp.bfloat16)
        total_sums = lax.psum(square_sums, "dp")
        own_sums = lax.dynamic_slice_in_dim(total_sums, dp_index * own_rows, own_rows, 0)
        proj_terms = lax.psum_scatter(
            jnp.dot(scaled, weights, preferred_element_type=jnp.float32).astype(jnp.bfloat16),
            "dp",
            scatter_dimension=0,
            tiled=True,
        ).astype(jnp.float32)
        inv_rms = lax.rsqrt(own_sums / D + epsilon)[:, None]
        projected = (proj_terms * inv_rms).astype(jnp.bfloat16)
        queries = projected[:, :head_cols].reshape(local_requests, BRANCH, kv_local, -1, HD)
        new_keys = projected[:, head_cols : head_cols + kv_cols].reshape(
            local_requests, BRANCH, kv_local, HD
        )
        new_values = projected[:, head_cols + kv_cols :].reshape(
            local_requests, BRANCH, kv_local, HD
        )
        tree_keys = tree_keys.at[:, tree_level * BRANCH : (tree_level + 1) * BRANCH].set(new_keys)
        tree_values = tree_values.at[:, tree_level * BRANCH : (tree_level + 1) * BRANCH].set(
            new_values
        )
        tree_mask = tree_mask_of(own_parents, tree_level)
        cache_scores = jnp.einsum(
            "rbkgd,rckd->rkgbc", queries, cache_keys, preferred_element_type=jnp.float32
        ) * HD ** (-0.5)
        tree_scores = jnp.einsum(
            "rbkgd,rtkd->rkgbt", queries, tree_keys, preferred_element_type=jnp.float32
        ) * HD ** (-0.5)
        cache_scores = jnp.where(cache_valid[:, None, None, None, :], cache_scores, masked_score)
        tree_scores = jnp.where(tree_mask[:, None, None, :, :], tree_scores, masked_score)
        row_max = jnp.maximum(jnp.max(cache_scores, axis=4), jnp.max(tree_scores, axis=4))[
            ..., None
        ]
        cache_exp = jnp.exp(cache_scores - row_max)
        tree_exp = jnp.exp(tree_scores - row_max)
        denominator = jnp.sum(cache_exp, axis=4, keepdims=True) + jnp.sum(
            tree_exp, axis=4, keepdims=True
        )
        cache_weights = (cache_exp / denominator).astype(jnp.bfloat16)
        tree_weights = (tree_exp / denominator).astype(jnp.bfloat16)
        mixed = jnp.einsum(
            "rkgbc,rckd->rbkgd", cache_weights, cache_values, preferred_element_type=jnp.float32
        )
        mixed = mixed + jnp.einsum(
            "rkgbt,rtkd->rbkgd", tree_weights, tree_values, preferred_element_type=jnp.float32
        )
        attended = mixed.reshape(own_rows, head_cols).astype(jnp.bfloat16)
        partial_out = jnp.dot(
            lax.all_gather(attended, "dp", axis=0, tiled=True),
            w_out,
            preferred_element_type=jnp.float32,
        )
        share_sums = lax.psum_scatter(
            partial_out.astype(jnp.bfloat16), "tensor", scatter_dimension=1, tiled=True
        ).astype(jnp.float32)
        residual = lax.dynamic_slice_in_dim(flat_state, tensor_index * share_cols, share_cols, 1)
        fresh_share = (residual + share_sums).astype(jnp.bfloat16)
        if tree_level + 1 < DEPTHS:
            gathered = lax.all_gather(fresh_share, "tensor", axis=1, tiled=True)
            previous = gathered.reshape(request_count, BRANCH, feat_cols)
        results.append(fresh_share.reshape(request_count, BRANCH, share_cols))
    return jnp.stack(results, axis=1)


MESH = pl.DeviceIdType.MESH


def dot32(a, b):
    return jnp.dot(a, b, preferred_element_type=jnp.float32)


def dot32_t(a, b):
    return lax.dot_general(a, b, (((1,), (1,)), ((), ())), preferred_element_type=jnp.float32)


def timetable(n, chunks):
    per = chunks // n
    jobs = []
    for s in range(chunks):
        for hops in range(1, n - 1):
            jobs.append((HOP * hops + PACE * s, hops, s))
        if s % per == per - 1:
            jobs.append((HOP * (n - 1) + PACE * s + SLACK, n - 1, s // per))
    phases = ([], [], [])
    for time, hops, s in jobs:
        age, when = 1, time
        while when >= PERIOD:
            age, when = age + 1, when - PERIOD
        phase = 0 if when < PERIOD - TURN else 1 if when < PERIOD - TURN + PROJ_TRIP else 2
        if age > BATCHES or (age == BATCHES and phase > 0):
            age, phase, when = BATCHES, 0, when + PERIOD * (age - BATCHES)
        phases[phase].append((when, -age, hops, s))
    return [[(-age, hops, s) for _, age, hops, s in sorted(phase)] for phase in phases]


def tree_kernel(
    n,
    m,
    root_ref,
    emb_hbm,
    hot_ref,
    len_ref,
    cache_hbm,
    gain_ref,
    wq_hbm,
    wkv_hbm,
    wo_hbm,
    out_ref,
    emb,
    cache,
    wq,
    wkv,
    wo,
    scaled,
    state,
    part,
    right_send,
    right_recv,
    left_send,
    left_recv,
    proj,
    proj_send,
    proj_recv,
    squares,
    sums_recv,
    tree_keys,
    tree_values,
    tree_mask,
    att,
    load_sem,
    right_ssem,
    right_rsem,
    left_ssem,
    left_rsem,
    proj_ssem,
    proj_rsem,
    dsum_ssem,
    dsum_rsem,
    att_ssem,
    att_rsem,
):
    t = lax.axis_index("tensor")
    d = lax.axis_index("dp")
    requests, feat = root_ref.shape
    own_requests = requests // m
    part_requests = own_requests // BATCHES
    own = part_requests * BRANCH
    rows = own * m
    head_cols = wq.shape[1]
    heads = head_cols // HD
    steps = BATCHES * DEPTHS
    chunks, _, width = right_send.shape[1:]
    per = chunks // n
    tail = steps - BATCHES

    def cols_of(c, count=1):
        return slice(c * width, (c + count) * width)

    def batch_rows(b):
        return [pl.ds(k * own_requests + b * part_requests, part_requests) for k in range(m)]

    def joined(blocks, columns):
        return jnp.concatenate(blocks, axis=0).astype(jnp.float32).reshape(rows, columns)

    loads = [
        pltpu.make_async_copy(emb_hbm.at[:, 0], emb.at[0], load_sem.at[0]),
        pltpu.make_async_copy(wq_hbm, wq, load_sem.at[1]),
        pltpu.make_async_copy(wkv_hbm, wkv, load_sem.at[2]),
        pltpu.make_async_copy(cache_hbm, cache, load_sem.at[3]),
    ]
    for s in range(n):
        columns = slice(s * per * width, (s + 1) * per * width)
        loads.append(pltpu.make_async_copy(wo_hbm.at[:, columns], wo.at[s], load_sem.at[4 + s]))
    for e in range(1, DEPTHS):
        loads.append(
            pltpu.make_async_copy(emb_hbm.at[:, e], emb.at[e], load_sem.at[3 + n + e])
        )
    for load in loads:
        load.start()

    dp_to = [lax.rem(d + k, m) for k in range(1, m)]

    barrier = pltpu.get_barrier_semaphore()
    for peer in dp_to:
        pl.semaphore_signal(barrier, inc=1, device_id={"dp": peer}, device_id_type=MESH)

    for k in range(1, n):
        peer = lax.rem(t + k, n)
        pl.semaphore_signal(barrier, inc=1, device_id={"tensor": peer}, device_id_type=MESH)

    def right_copy(p, c):
        return pltpu.make_async_remote_copy(
            src_ref=right_send.at[p, c],
            dst_ref=right_recv.at[p, c],
            send_sem=right_ssem.at[p, c],
            recv_sem=right_rsem.at[p, c],
            device_id={"tensor": lax.rem(t + 1, n)},
            device_id_type=MESH,
        )

    def left_copy(p, c):
        return pltpu.make_async_remote_copy(
            src_ref=left_send.at[p, c],
            dst_ref=left_recv.at[p, c],
            send_sem=left_ssem.at[p, c],
            recv_sem=left_rsem.at[p, c],
            device_id={"tensor": lax.rem(t + n - 1, n)},
            device_id_type=MESH,
        )

    def proj_copy(i, k):
        return pltpu.make_async_remote_copy(
            src_ref=proj_send.at[i, dp_to[k]],
            dst_ref=proj_recv.at[i, k],
            send_sem=proj_ssem.at[i, k],
            recv_sem=proj_rsem.at[i, k],
            device_id={"dp": dp_to[k]},
            device_id_type=MESH,
        )

    def dsum_copy(i, k):
        return pltpu.make_async_remote_copy(
            src_ref=squares.at[i, dp_to[k]],
            dst_ref=sums_recv.at[i, k],
            send_sem=dsum_ssem.at[i, k],
            recv_sem=dsum_rsem.at[i, k],
            device_id={"dp": dp_to[k]},
            device_id_type=MESH,
        )

    def att_copy(i, k):
        return pltpu.make_async_remote_copy(
            src_ref=att.at[i, d],
            dst_ref=att.at[i, d],
            send_sem=att_ssem.at[i, k],
            recv_sem=att_rsem.at[i, k],
            device_id={"dp": dp_to[k]},
            device_id_type=MESH,
        )

    def right_limit(p):
        return jnp.where(p < tail, chunks, (n - 1 - t) * per)

    def left_limit(p):
        return jnp.where(p < tail, chunks, t * per)

    def right_chunk(p, s):
        return jnp.where(p < tail, s, chunks - 1 - s)

    def relay_right(p, s):
        @pl.when(s < right_limit(p))
        def _():
            c = right_chunk(p, s)
            right_copy(p, c).wait_recv()
            block = part[lax.rem(p, BATCHES), c] + right_recv[p, c].astype(jnp.float32)
            right_send[p, c] = block.astype(jnp.bfloat16)
            right_copy(p, c).start()

    def relay_left(p, s):
        @pl.when(s < left_limit(p))
        def _():
            left_copy(p, s).wait_recv()
            block = part[lax.rem(p, BATCHES), s] + left_recv[p, s].astype(jnp.float32)
            left_send[p, s] = block.astype(jnp.bfloat16)
            left_copy(p, s).start()

    def relays(p, hops, s):
        for place in range(1, n - 1):
            if hops not in (place, n - 1 - place):
                continue

            @pl.when((t == place) & (p >= 0))
            def _():
                if hops == place:
                    relay_right(p, s)
                if hops == n - 1 - place:
                    relay_left(p, s)

    def product(b, c, count, first):
        block = scaled[b, :, cols_of(c, count)]
        left, right = dot32(block, wq[cols_of(c, count)]), dot32(block, wkv[cols_of(c, count)])
        if first:
            proj[b, :, :head_cols] = left
            proj[b, :, head_cols:] = right
        else:
            proj[b, :, :head_cols] += left
            proj[b, :, head_cols:] += right

    def feed(i, c, node):
        b = lax.rem(i, BATCHES)
        state[b, c] = node
        gain = gain_ref[:, cols_of(c)].astype(jnp.float32)
        scaled[b, :, cols_of(c)] = (node * gain).astype(jnp.bfloat16)
        folded = jnp.zeros((rows, HD), jnp.float32)
        for low in range(0, width, HD):
            piece = node[:, low : low + HD]
            folded = folded + piece * piece
        folded = folded.reshape(m, own, HD)
        if c == 0:
            squares[i] = folded
        else:
            squares[i] += folded

    def keep(e, b, value, local):
        for k, r in enumerate(batch_rows(b)):
            out_ref[r, pl.ds(e, 1), :, local * width : (local + 1) * width] = (
                value[k * own : (k + 1) * own].reshape(part_requests, 1, BRANCH, width)
            )

    def finish(p, seg):
        b = lax.rem(p, BATCHES)
        e = p // BATCHES
        group = range(seg * per, (seg + 1) * per)

        @pl.when(t == 0)
        def _():
            for c in group:
                left_copy(p, c).wait_recv()

        @pl.when(t == n - 1)
        def _():
            for c in group:
                right_copy(p, c).wait_recv()

        whole = [
            (
                state[b, c]
                + part[b, c]
                + right_recv[p, c].astype(jnp.float32)
                + left_recv[p, c].astype(jnp.float32)
            ).astype(jnp.bfloat16)
            for c in group
        ]
        hot = hot_ref[p]
        for c, fresh in zip(group, whole):
            embeds = joined([emb[e + 1, r, :, cols_of(c)] for r in batch_rows(b)], width)
            feed(p + BATCHES, c, dot32(hot, fresh) + embeds)
        product(b, seg * per, per, seg == 0)

        @pl.when(t == seg)
        def _():
            for c, fresh in zip(group, whole):
                keep(e, b, fresh, c % per)

    def finish_last(p):
        b = lax.rem(p, BATCHES)
        e = p // BATCHES
        for local in range(per):
            c = t * per + local

            @pl.when(t > 0)
            def _():
                right_copy(p, c).wait_recv()

            @pl.when(t < n - 1)
            def _():
                left_copy(p, c).wait_recv()

            total = (
                state[b, c]
                + part[b, c]
                + right_recv[p, c].astype(jnp.float32)
                + left_recv[p, c].astype(jnp.float32)
            )
            keep(e, b, total.astype(jnp.bfloat16), local)

    row_id = lax.broadcasted_iota(jnp.int32, (rows, requests), 0)
    request_id = lax.broadcasted_iota(jnp.int32, (rows, requests), 1)

    def first_states(b):
        place = row_id // BRANCH
        request = (
            place // part_requests * own_requests + b * part_requests + place % part_requests
        )
        root_hot = (request == request_id).astype(jnp.bfloat16)
        for c in range(chunks):
            embeds = joined([emb[0, r, :, cols_of(c)] for r in batch_rows(b)], width)
            feed(b, c, dot32(root_hot, root_ref[:, cols_of(c)]) + embeds)

    def first_product(b):
        for c in range(0, chunks, per):
            product(b, c, per, c == 0)

    tree_keys[...] = jnp.zeros_like(tree_keys)
    tree_values[...] = jnp.zeros_like(tree_values)
    tree_mask[...] = jnp.zeros_like(tree_mask)

    @pl.when(t == 0)
    def _():
        right_recv[...] = jnp.zeros_like(right_recv)

    @pl.when(t == n - 1)
    def _():
        left_recv[...] = jnp.zeros_like(left_recv)

    loads[0].wait()
    first_states(0)
    loads[1].wait()
    loads[2].wait()
    first_product(0)
    pl.semaphore_wait(barrier, m + n - 2)

    timed = timetable(n, chunks)

    def run(i, phase):
        for age, hops, s in timed[phase]:
            p = i - age
            if hops < n - 1:
                relays(p, hops, s)
            else:

                @pl.when((p >= 0) & (p < tail))
                def _():
                    finish(p, s)

    def relay_rest(p):
        for age in range(max(1, steps - p), BATCHES + 1):
            for phase in range(3):
                for job_age, hops, s in timed[phase]:
                    if job_age == age and hops < n - 1:
                        relays(p, hops, s)

    def step(i, carry):
        b = lax.rem(i, BATCHES)
        e = i // BATCHES

        with jax.named_scope("A_tail"):

            run(i, 0)

        with jax.named_scope("B_send"):
            for k in range(m):
                proj_send[i, k] = proj[b, k * own : (k + 1) * own].astype(jnp.bfloat16)
            for k in range(m - 1):
                proj_copy(i, k).start()
                dsum_copy(i, k).start()

        with jax.named_scope("C_mid"):

            @pl.when(i < BATCHES - 1)
            def _():
                first_states(i + 1)
                first_product(i + 1)

            run(i, 1)
            own_row = lax.broadcasted_iota(jnp.int32, (own, DEPTHS * own), 0)
            own_col = lax.broadcasted_iota(jnp.int32, (own, DEPTHS * own), 1)
            itself = (own_col == own_row + e * own).astype(jnp.float32)
            own_rows = pl.ds(pl.multiple_of(d * own, own), own)
            mask_now = itself + dot32(hot_ref[jnp.maximum(i - BATCHES, 0), own_rows], tree_mask[b])
            tree_mask[b, own_rows] = mask_now.astype(jnp.bfloat16)

        projected = proj[b, pl.ds(pl.multiple_of(d * own, own), own)]
        summed = squares[i, d]
        with jax.named_scope("D_projwait"):
            for k in range(m - 1):
                proj_copy(i, k).wait_recv()
                dsum_copy(i, k).wait_recv()
                projected = projected + proj_recv[i, k].astype(jnp.float32)
                summed = summed + sums_recv[i, k]

        with jax.named_scope("E_attn"):
            inv_rms = lax.rsqrt(jnp.sum(summed, axis=1, keepdims=True) / (feat * m) + epsilon)
            projected = projected * inv_rms
            queries = jnp.concatenate(
                [
                    projected[:, h * HD : (h + 1) * HD].reshape(part_requests, 1, BRANCH, HD)
                    for h in range(heads)
                ],
                axis=1,
            ).reshape(own * heads, HD).astype(jnp.bfloat16)
            now = pl.ds(pl.multiple_of(e * own, own), own)
            tree_keys[b, now] = projected[:, head_cols : head_cols + HD].astype(jnp.bfloat16)
            tree_values[b, now] = projected[:, head_cols + HD :].astype(jnp.bfloat16)

            @pl.when(i == 0)
            def _():
                loads[3].wait()

            tall = heads * BRANCH
            tree_scores = dot32_t(queries, tree_keys[b]) * HD ** (-0.5)
            allowed = jnp.broadcast_to(
                mask_now.reshape(part_requests, 1, BRANCH, DEPTHS * own),
                (part_requests, heads, BRANCH, DEPTHS * own),
            ).reshape(own * heads, DEPTHS * own)
            tree_scores = jnp.where(allowed > 0.5, tree_scores, masked_score)
            cache_scores = []
            position = lax.broadcasted_iota(jnp.int32, (tall, CACHE), 1)
            for r in range(part_requests):
                request = b * part_requests + r
                scores = dot32_t(queries[r * tall : (r + 1) * tall], cache[request, 0])
                scores = scores * HD ** (-0.5)
                cache_scores.append(jnp.where(position < len_ref[request], scores, masked_score))
            cache_scores = jnp.concatenate(cache_scores, axis=0)
            row_max = jnp.maximum(
                jnp.max(cache_scores, axis=1, keepdims=True),
                jnp.max(tree_scores, axis=1, keepdims=True),
            )
            cache_exp = jnp.exp(cache_scores - row_max)
            tree_exp = jnp.exp(tree_scores - row_max)
            denominator = jnp.sum(cache_exp, axis=1, keepdims=True) + jnp.sum(
                tree_exp, axis=1, keepdims=True
            )
            cache_weights = (cache_exp / denominator).astype(jnp.bfloat16)
            tree_weights = (tree_exp / denominator).astype(jnp.bfloat16)
            mixed = jnp.concatenate(
                [
                    dot32(cache_weights[r * tall : (r + 1) * tall], cache[b * part_requests + r, 1])
                    for r in range(part_requests)
                ],
                axis=0,
            ) + dot32(tree_weights, tree_values[b])
            mixed = mixed.reshape(part_requests, heads, BRANCH, HD)
            for h in range(heads):
                att[i, d, :, h * HD : (h + 1) * HD] = (
                    mixed[:, h].reshape(own, HD).astype(jnp.bfloat16)
                )
            for k in range(m - 1):
                att_copy(i, k).start()

        with jax.named_scope("F_mid"):
            run(i, 2)

        with jax.named_scope("G_attwait"):
            for k in range(m - 1):
                att_copy(i, k).wait_recv()

            @pl.when(i == 0)
            def _():
                for load in loads[4:]:
                    load.wait()

        with jax.named_scope("H_out"):
            attended = att[i].reshape(rows, head_cols)
            last = i >= tail
            for q in range(n):
                seg = jnp.where(last & (t == 0), n - 1 - q, q)
                block = dot32(attended, wo[seg])
                for j in range(per):
                    part[b, seg * per + j] = block[:, j * width : (j + 1) * width]

                @pl.when((t == 0) & (q * per < right_limit(i)))
                def _():
                    for j in range(per):
                        c = seg * per + jnp.where(last, per - 1 - j, j)
                        right_send[i, c] = part[b, c].astype(jnp.bfloat16)
                        right_copy(i, c).start()

                @pl.when((t == n - 1) & (q * per < left_limit(i)))
                def _():
                    for j in range(per):
                        c = seg * per + j
                        left_send[i, c] = part[b, c].astype(jnp.bfloat16)
                        left_copy(i, c).start()

        return carry

    lax.fori_loop(0, steps, step, 0)
    with jax.named_scope("Z_tail"):
        for p in range(tail, steps):
            relay_rest(p)
            finish_last(p)

    def drain(i, carry):
        for k in range(m - 1):
            proj_copy(i, k).wait_send()
            dsum_copy(i, k).wait_send()
            att_copy(i, k).wait_send()
        for s in range(chunks):

            @pl.when((t < n - 1) & (s < right_limit(i)))
            def _():
                right_copy(i, right_chunk(i, s)).wait_send()

            @pl.when((t > 0) & (s < left_limit(i)))
            def _():
                left_copy(i, s).wait_send()

        return carry

    with jax.named_scope("Z_drain"):
        lax.fori_loop(0, steps, drain, 0)


def kernel_shards(
    root_features,
    branch_embeds,
    parents,
    cache_lengths,
    cache_kv,
    norm_gain,
    w_query,
    w_keyval,
    w_out,
):
    n = lax.axis_size("tensor")
    m = lax.axis_size("dp")
    requests, feat = root_features.shape
    own_requests = cache_lengths.shape[0]
    part_requests = own_requests // BATCHES
    own = part_requests * BRANCH
    rows = own * m
    steps = BATCHES * DEPTHS
    head_cols = w_query.shape[1]
    proj_cols = head_cols + 2 * HD
    chunks = n * PER
    width = feat // chunks

    def one_hots(table):
        count = rows
        split = table.reshape(m, BATCHES, part_requests, DEPTHS - 1, BRANCH)
        split = jnp.transpose(split, (3, 1, 0, 2, 4)).reshape((DEPTHS - 1) * BATCHES, count)
        lane = jnp.arange(count, dtype=jnp.int32)
        index = split + (lane // BRANCH * BRANCH)[None, :]
        return (index[:, :, None] == lane[None, None, :]).astype(jnp.bfloat16)

    hot = one_hots(parents)
    bf16, f32 = jnp.bfloat16, jnp.float32
    vmem = pl.BlockSpec(memory_space=pltpu.VMEM)
    smem = pl.BlockSpec(memory_space=pltpu.SMEM)
    hbm = pl.BlockSpec(memory_space=pl.ANY)
    dma = pltpu.SemaphoreType.DMA
    passing = pltpu.VMEM((steps, chunks, rows, width), bf16)
    return pl.pallas_call(
        functools.partial(tree_kernel, n, m),
        out_shape=jax.ShapeDtypeStruct((requests, DEPTHS, BRANCH, feat // n), bf16),
        in_specs=[vmem, hbm, vmem, smem, hbm, vmem, hbm, hbm, hbm],
        out_specs=vmem,
        scratch_shapes=[
            pltpu.VMEM((DEPTHS, requests, BRANCH, feat), bf16),
            pltpu.VMEM(cache_kv.shape, bf16),
            pltpu.VMEM((feat, head_cols), bf16),
            pltpu.VMEM((feat, 2 * HD), bf16),
            pltpu.VMEM((n, head_cols, feat // n), bf16),
            pltpu.VMEM((BATCHES, rows, feat), bf16),
            pltpu.VMEM((BATCHES, chunks, rows, width), f32),
            pltpu.VMEM((BATCHES, chunks, rows, width), f32),
            passing,
            passing,
            passing,
            passing,
            pltpu.VMEM((BATCHES, rows, proj_cols), f32),
            pltpu.VMEM((steps, m, own, proj_cols), bf16),
            pltpu.VMEM((steps, m - 1, own, proj_cols), bf16),
            pltpu.VMEM((steps, m, own, HD), f32),
            pltpu.VMEM((steps, m - 1, own, HD), f32),
            pltpu.VMEM((BATCHES, DEPTHS * own, HD), bf16),
            pltpu.VMEM((BATCHES, DEPTHS * own, HD), bf16),
            pltpu.VMEM((BATCHES, rows, DEPTHS * own), bf16),
            pltpu.VMEM((steps, m, own, head_cols), bf16),
            dma((3 + n + DEPTHS,)),
            dma((steps, chunks)),
            dma((steps, chunks)),
            dma((steps, chunks)),
            dma((steps, chunks)),
            dma((steps, m - 1)),
            dma((steps, m - 1)),
            dma((steps, m - 1)),
            dma((steps, m - 1)),
            dma((steps, m - 1)),
            dma((steps, m - 1)),
        ],
        compiler_params=pltpu.CompilerParams(
            collective_id=0, has_side_effects=True, vmem_limit_bytes=60 * 1024 * 1024
        ),
    )(
        root_features,
        branch_embeds,
        hot,
        cache_lengths,
        cache_kv,
        norm_gain[None, :],
        w_query,
        w_keyval.reshape(feat, 2 * HD),
        w_out,
    )


def solution(mesh):
    in_line = 1 < mesh.shape["tensor"] <= 8 and mesh.shape["dp"] > 1
    return jax.shard_map(
        kernel_shards if in_line else shards,
        mesh=mesh,
        in_specs=(
            P("groups", "dp"),
            P("groups", None, None, "dp"),
            P("groups", None, None),
            P(("groups", "dp")),
            P(("groups", "dp"), None, None, "tensor"),
            P("dp"),
            P("dp", "tensor"),
            P("dp", None, "tensor"),
            P("tensor", "dp"),
        ),
        out_specs=P("groups", None, None, ("dp", "tensor")),
        check_vma=False,
    )
```

time: 163 us -> 141 us (0.87)
  Pallas kernels: 155 us -> 132 us
    pallas_call x1, Pallas kernels: 155 us -> 132 us  [kernel_shards(): pl.pallas_call(functools.partial(tree_kernel, n, m), out_shape=jax.ShapeD...]
where the time goes in v1:
time: 141 us
  Pallas kernels  132 us (94%)
  local copies, waits for them, and re-layouts  7.69 us (5%)
    pallas_call x1, Pallas kernels, kernel_shards(): pl.pallas_call(functools.partial(tree_kernel, n, m), out_shape=jax.ShapeD...  132 us
    unnamed x3, local copies, waits for them, and re-layouts  6.28 us

profile of v1, /device:TPU:0, one launch (start us, length us, event | category | flops | bytes accessed | tf_op | source)
XLA Modules:
  0.0 140.7 jit_solution(14510365679516261242)
XLA Ops:
  0.0 1.3 broadcast_in_dim.2.gain_ref
  1.3 0.8 copy.12
  2.1 0.1 reshape.41
  2.2 0.8 fusion.hot_ref
  3.0 3.2 %copy.16 = bf16[512,8,2,128]{3,1,2,0:T(8,128)(2,1)} copy(bf16[512,8,2,128]{3,2,1,0:T(2,128)(2,1)} %bitcast.8) | data formatting | bytes 4194304
  6.2 132.2 %shard_map.91 = bf16[16,4,8,1024]{3,2,1,0:T(8,128)(2,1)} custom-call(bf16[16,4096]{1,0:T(8,128)(2,1)} %root_ref.1, bf16[16,4,8,4096]{3,2,1,0:T(8,128)(2,1)} %emb_hbm.1, bf16[6,64,64]{2,1,0:T(8,128)(2,1)} %fusion.hot_ref, s32[4]{0:T(128)} %len_ref.1, bf16[4,2,512,128]{3,2,1,0:T(8,128)(2,1)} %cache_hbm.1, bf16[1,4096]{1,0:T(2,128)(2,1)} %broadcast_in_dim.2.gain_ref, ...), custom_call_target="tpu_custom_call" | custom-call | tf_op jit(solution)/shard_map/pallas_call | solution.py:716
  138.4 2.3 %copy.18 = bf16[16,4,8,1024]{3,2,1,0:T(8,128)(2,1)} copy(bf16[16,4,8,1024]{3,2,1,0:T(8,128)(2,1)} %shard_map.91) | data formatting | bytes 2097152
  (3 shorter events, 0.0 us)

commit v2 on v1

--- a/solution.py
+++ b/solution.py
@@ -20,6 +20,7 @@
 TURN = 7.2
 PROJ_TRIP = 2.9
 SLACK = 0.5
+HOLD = 1.25
 
 
 epsilon = 1e-05
@@ -173,14 +174,16 @@
             jobs.append((HOP * hops + PACE * s, hops, s))
         if s % per == per - 1:
             jobs.append((HOP * (n - 1) + PACE * s + SLACK, n - 1, s // per))
-    phases = ([], [], [])
-    for time, hops, s in jobs:
-        age, when = 1, time
+    phases = [[] for _ in range(3 + n)]
+    for when, hops, s in jobs:
+        age = 1
         while when >= PERIOD:
             age, when = age + 1, when - PERIOD
         phase = 0 if when < PERIOD - TURN else 1 if when < PERIOD - TURN + PROJ_TRIP else 2
         if age > BATCHES or (age == BATCHES and phase > 0):
             age, phase, when = BATCHES, 0, when + PERIOD * (age - BATCHES)
+        elif when < HOLD and age > 1 and hops < n - 1:
+            age, phase = age - 1, 3 + int(when * n / HOLD)
         phases[phase].append((when, -age, hops, s))
     return [[(-age, hops, s) for _, age, hops, s in sorted(phase)] for phase in phases]
 
@@ -190,7 +193,7 @@
     m,
     root_ref,
     emb_hbm,
-    hot_ref,
+    parents_ref,
     len_ref,
     cache_hbm,
     gain_ref,
@@ -198,9 +201,13 @@
     wkv_hbm,
     wo_hbm,
     out_ref,
+    hot,
+    gain,
     emb,
     cache,
     wq,
+    pairs,
+    apart,
     wkv,
     wo,
     scaled,
@@ -256,8 +263,8 @@
 
     loads = [
         pltpu.make_async_copy(emb_hbm.at[:, 0], emb.at[0], load_sem.at[0]),
+        pltpu.make_async_copy(wkv_hbm, pairs, load_sem.at[2]),
         pltpu.make_async_copy(wq_hbm, wq, load_sem.at[1]),
-        pltpu.make_async_copy(wkv_hbm, wkv, load_sem.at[2]),
         pltpu.make_async_copy(cache_hbm, cache, load_sem.at[3]),
     ]
     for s in range(n):
@@ -381,12 +388,13 @@
     def feed(i, c, node):
         b = lax.rem(i, BATCHES)
         state[b, c] = node
-        gain = gain_ref[:, cols_of(c)].astype(jnp.float32)
-        scaled[b, :, cols_of(c)] = (node * gain).astype(jnp.bfloat16)
         folded = jnp.zeros((rows, HD), jnp.float32)
         for low in range(0, width, HD):
             piece = node[:, low : low + HD]
             folded = folded + piece * piece
+            line = (c * width + low) // HD
+            fed = (piece * gain[line : line + 1]).astype(jnp.bfloat16)
+            scaled[b, :, line * HD : (line + 1) * HD] = fed
         folded = folded.reshape(m, own, HD)
         if c == 0:
             squares[i] = folded
@@ -423,10 +431,10 @@
             ).astype(jnp.bfloat16)
             for c in group
         ]
-        hot = hot_ref[p]
+        pick = hot[p]
         for c, fresh in zip(group, whole):
             embeds = joined([emb[e + 1, r, :, cols_of(c)] for r in batch_rows(b)], width)
-            feed(p + BATCHES, c, dot32(hot, fresh) + embeds)
+            feed(p + BATCHES, c, dot32(pick, fresh) + embeds)
         product(b, seg * per, per, seg == 0)
 
         @pl.when(t == seg)
@@ -485,11 +493,42 @@
     def _():
         left_recv[...] = jnp.zeros_like(left_recv)
 
-    loads[0].wait()
-    first_states(0)
-    loads[1].wait()
-    loads[2].wait()
-    first_product(0)
+    with jax.named_scope("Q_gain"):
+        gain[...] = gain_ref[...].astype(jnp.float32)
+        if True:
+            lane = lax.broadcasted_iota(jnp.int32, (BRANCH, rows), 1)
+            for e in range(DEPTHS - 1):
+                table = parents_ref[e]
+                for b in range(BATCHES):
+                    blocks = []
+                    for k in range(m):
+                        for q in range(part_requests):
+                            r = k * own_requests + b * part_requests + q
+                            base = (k * part_requests + q) * BRANCH
+                            blocks.append(lane == table[:, r : r + 1] + base)
+                    stacked = jnp.concatenate([x.astype(jnp.float32) for x in blocks], axis=0)
+                    hot[e * BATCHES + b] = stacked.astype(jnp.bfloat16)
+    with jax.named_scope("Q_emb"):
+        loads[0].wait()
+    with jax.named_scope("Q_first"):
+        first_states(0)
+    with jax.named_scope("Q_kvwait"):
+        loads[1].wait()
+    with jax.named_scope("Q_apart"):
+        block = apart.shape[0]
+
+        def split(j, carry):
+            apart[...] = pairs[pl.ds(pl.multiple_of(j * block, block), block)].astype(jnp.float32)
+            out = pl.ds(pl.multiple_of(j * (block // 2), block // 2), block // 2)
+            wkv[out, :HD] = apart[pl.ds(0, block // 2, stride=2)].astype(jnp.bfloat16)
+            wkv[out, HD:] = apart[pl.ds(1, block // 2, stride=2)].astype(jnp.bfloat16)
+            return carry
+
+        lax.fori_loop(0, 2 * feat // block, split, 0)
+    with jax.named_scope("Q_wqwait"):
+        loads[2].wait()
+    with jax.named_scope("Q_prod"):
+        first_product(0)
     pl.semaphore_wait(barrier, m + n - 2)
 
     timed = timetable(n, chunks)
@@ -507,7 +546,7 @@
 
     def relay_rest(p):
         for age in range(max(1, steps - p), BATCHES + 1):
-            for phase in range(3):
+            for phase in range(3 + n):
                 for job_age, hops, s in timed[phase]:
                     if job_age == age and hops < n - 1:
                         relays(p, hops, s)
@@ -539,7 +578,7 @@
             own_col = lax.broadcasted_iota(jnp.int32, (own, DEPTHS * own), 1)
             itself = (own_col == own_row + e * own).astype(jnp.float32)
             own_rows = pl.ds(pl.multiple_of(d * own, own), own)
-            mask_now = itself + dot32(hot_ref[jnp.maximum(i - BATCHES, 0), own_rows], tree_mask[b])
+            mask_now = itself + dot32(hot[jnp.maximum(i - BATCHES, 0), own_rows], tree_mask[b])
             tree_mask[b, own_rows] = mask_now.astype(jnp.bfloat16)
 
         projected = proj[b, pl.ds(pl.multiple_of(d * own, own), own)]
@@ -626,6 +665,8 @@
             attended = att[i].reshape(rows, head_cols)
             last = i >= tail
             for q in range(n):
+                if q > 0:
+                    run(i, 2 + q)
                 seg = jnp.where(last & (t == 0), n - 1 - q, q)
                 block = dot32(attended, wo[seg])
                 for j in range(per):
@@ -645,13 +686,8 @@
                         left_send[i, c] = part[b, c].astype(jnp.bfloat16)
                         left_copy(i, c).start()
 
+            run(i, 2 + n)
         return carry
-
-    lax.fori_loop(0, steps, step, 0)
-    with jax.named_scope("Z_tail"):
-        for p in range(tail, steps):
-            relay_rest(p)
-            finish_last(p)
 
     def drain(i, carry):
         for k in range(m - 1):
@@ -670,8 +706,15 @@
 
         return carry
 
-    with jax.named_scope("Z_drain"):
-        lax.fori_loop(0, steps, drain, 0)
+    lax.fori_loop(0, steps, step, 0)
+    with jax.named_scope("Z_tail"):
+        for p in range(tail, steps - 1):
+            relay_rest(p)
+            finish_last(p)
+        relay_rest(steps - 1)
+        lax.fori_loop(0, steps - 1, drain, 0)
+        finish_last(steps - 1)
+        drain(steps - 1, 0)
 
 
 def kernel_shards(
@@ -698,15 +741,6 @@
     chunks = n * PER
     width = feat // chunks
 
-    def one_hots(table):
-        count = rows
-        split = table.reshape(m, BATCHES, part_requests, DEPTHS - 1, BRANCH)
-        split = jnp.transpose(split, (3, 1, 0, 2, 4)).reshape((DEPTHS - 1) * BATCHES, count)
-        lane = jnp.arange(count, dtype=jnp.int32)
-        index = split + (lane // BRANCH * BRANCH)[None, :]
-        return (index[:, :, None] == lane[None, None, :]).astype(jnp.bfloat16)
-
-    hot = one_hots(parents)
     bf16, f32 = jnp.bfloat16, jnp.float32
     vmem = pl.BlockSpec(memory_space=pltpu.VMEM)
     smem = pl.BlockSpec(memory_space=pltpu.SMEM)
@@ -719,9 +753,13 @@
         in_specs=[vmem, hbm, vmem, smem, hbm, vmem, hbm, hbm, hbm],
         out_specs=vmem,
         scratch_shapes=[
+            pltpu.VMEM(((DEPTHS - 1) * BATCHES, rows, rows), bf16),
+            pltpu.VMEM((feat // HD, HD), f32),
             pltpu.VMEM((DEPTHS, requests, BRANCH, feat), bf16),
             pltpu.VMEM(cache_kv.shape, bf16),
             pltpu.VMEM((feat, head_cols), bf16),
+            pltpu.VMEM((2 * feat, HD), bf16),
+            pltpu.VMEM((1024, HD), f32),
             pltpu.VMEM((feat, 2 * HD), bf16),
             pltpu.VMEM((n, head_cols, feat // n), bf16),
             pltpu.VMEM((BATCHES, rows, feat), bf16),
@@ -758,12 +796,12 @@
     )(
         root_features,
         branch_embeds,
-        hot,
+        jnp.transpose(parents, (1, 2, 0)),
         cache_lengths,
         cache_kv,
-        norm_gain[None, :],
+        norm_gain.reshape(feat // HD, HD),
         w_query,
-        w_keyval.reshape(feat, 2 * HD),
+        w_keyval.reshape(2 * feat, HD),
         w_out,
     )
 

time: 141 us -> 132 us (0.936)
  local copies, waits for them, and re-layouts: 7.69 us -> 2.29 us
  Pallas kernels: 132 us -> 129 us
    unnamed x3 -> x1, local copies, waits for them, and re-layouts: 6.28 us -> 2.29 us
    pallas_call x1, Pallas kernels: 132 us -> 129 us  [kernel_shards(): pl.pallas_call(functools.partial(tree_kernel, n, m), out_shape=jax.ShapeD...]
where the time goes in v2:
time: 132 us
  Pallas kernels  129 us (98%)
  local copies, waits for them, and re-layouts  2.29 us (2%)
    pallas_call x1, Pallas kernels, kernel_shards(): pl.pallas_call(functools.partial(tree_kernel, n, m), out_shape=jax.ShapeD...  129 us

profile of v2, /device:TPU:0, one launch (start us, length us, event | category | flops | bytes accessed | tf_op | source)
XLA Modules:
  0.0 131.5 jit_solution(12996109733480986651)
XLA Ops:
  0.0 129.2 %shard_map.91 = bf16[16,4,8,1024]{3,2,1,0:T(8,128)(2,1)} custom-call(bf16[16,4096]{1,0:T(8,128)(2,1)} %root_ref.1, bf16[16,4,8,4096]{3,2,1,0:T(8,128)(2,1)} %emb_hbm.1, s32[3,8,16]{2,1,0:T(8,128)} %bitcast.4, s32[4]{0:T(128)} %len_ref.1, bf16[4,2,512,128]{3,2,1,0:T(8,128)(2,1)} %cache_hbm.1, bf16[32,128]{1,0:T(8,128)(2,1)} %bitcast.5, ...), custom_call_target="tpu_custom_call" | custom-call | tf_op jit(solution)/shard_map/pallas_call | solution.py:750
  129.2 2.3 %copy.11 = bf16[16,4,8,1024]{3,2,1,0:T(8,128)(2,1)} copy(bf16[16,4,8,1024]{3,2,1,0:T(8,128)(2,1)} %shard_map.91) | data formatting | bytes 2097152
